TPU v7x, 128 devices: a whole 4x4x4 slice. The times are simulated.
128 devices in a mesh: row: 16 (over y, z), col: 8 (over x, core).
Axes of the slice: x: 4, y: 4, z: 4, core: 2. Of those that a mesh axis runs over, the one named last changes fastest.
Arguments:
- fock_matrix: bfloat16 [3072, 3072], P('row', 'col'), as said below
- density: bfloat16 [3072, 3072], P('row', 'col'), as said below
- margin: bfloat16 [3072, 3072], P('row', 'col'), as said below
- fill_patterns: int32 [3, 96, 96], P(None, 'row', 'col'), may hold values from 0 to 1, as said below
- first_filters: int32 [3, 96, 96], P(None, 'row', 'col'), may hold values from 0 to 1, as said below
- owner_order: int32 [96], replicated, may hold values from 0 to 95, as said below
- second_filters: int32 [7, 96, 96], P(None, 'row', 'col'), may hold values from 0 to 1, as said below
Outputs:
- evolved: bfloat16 [3072, 3072], P('row', 'col')
Inputs may be any that keep to these rules, and one draw needn't show every extreme that they name: `fock_matrix`: Symmetric. `density`: Symmetric. `margin`: Symmetric, with unit diagonal. `fill_patterns`: each entry says whether a block is kept; each pattern is symmetric and keeps every diagonal block. `first_filters`: each entry says whether a block of the product is kept; each filter is symmetric and keeps every diagonal block. `second_filters`: each entry says whether a block of the product is kept, indexed in owner order; each filter is symmetric and keeps every diagonal block. `owner_order`: A permutation of the 96 block indices.
All inputs are finite; a program needn't handle non-finite values.
Results may differ from a plain program's by a relative error of at most 0.012.
Values may be sent and summed in bfloat16 or wider, within the bound.
A program may use at most 64 MiB of HBM per device.

v0:
```python
import jax
import jax.numpy as jnp
from jax import lax
from jax.sharding import PartitionSpec as P

BLK = 32
TERMS = 6
SQUARINGS = 2


def expand(mask, values):
    row_blocks = mask.shape[0]
    column_blocks = mask.shape[1]
    shaped = values.reshape(row_blocks, BLK, column_blocks, BLK) * mask[:, None, :, None].astype(
        values.dtype
    )
    return shaped.reshape(values.shape)


def panel_rows(matrix):
    return lax.all_gather(matrix, "col", axis=1, tiled=True)


def panel_times(row_panel, matrix):
    return jnp.dot(
        row_panel,
        lax.all_gather(matrix, "row", axis=0, tiled=True),
        preferred_element_type=jnp.float32,
    )


def reorder(generator, owner_order):
    row_blocks = generator.shape[0] // BLK
    column_blocks = generator.shape[1] // BLK
    wanted_rows = lax.dynamic_slice_in_dim(
        owner_order, lax.axis_index("row") * row_blocks, row_blocks
    )
    wanted_columns = lax.dynamic_slice_in_dim(
        owner_order, lax.axis_index("col") * column_blocks, column_blocks
    )
    segment = lax.all_gather(generator, "row", axis=0, tiled=True)
    arriving = segment.shape[0] // BLK
    source = jnp.arange(arriving, dtype=jnp.int32)
    select = (wanted_rows[:, None] == source[None, :]).astype(jnp.bfloat16)
    flattened = segment.reshape(arriving, -1)
    by_rows = jnp.dot(select, flattened, preferred_element_type=jnp.float32)
    by_rows = by_rows.reshape(generator.shape).astype(jnp.bfloat16)
    segment = lax.all_gather(by_rows, "col", axis=1, tiled=True)
    arriving = segment.shape[1] // BLK
    source = jnp.arange(arriving, dtype=jnp.int32)
    select = (source[:, None] == wanted_columns[None, :]).astype(jnp.bfloat16)
    shaped = segment.reshape(segment.shape[0], arriving, BLK)
    placed = jnp.einsum("pjk,ji->pik", shaped, select, preferred_element_type=jnp.float32)
    return placed.reshape(generator.shape).astype(jnp.bfloat16)


def on_device(
    fock_matrix, density, margin, fill_patterns, first_filters, owner_order, second_filters
):
    masked_fock = expand(fill_patterns[0], fock_matrix)
    masked_density = expand(fill_patterns[1], density)
    masked_margin = expand(fill_patterns[2], margin)
    fock_density = expand(
        first_filters[0], panel_times(panel_rows(masked_fock), masked_density)
    ).astype(jnp.bfloat16)
    margin_density = expand(
        first_filters[1], panel_times(panel_rows(masked_margin), masked_density)
    ).astype(jnp.bfloat16)
    generator = panel_times(panel_rows(fock_density), masked_margin) - panel_times(
        panel_rows(margin_density), masked_fock
    )
    generator = expand(first_filters[2], generator).astype(jnp.bfloat16)
    reordered = reorder(generator, owner_order)
    scaled = (reordered.astype(jnp.float32) * 0.25).astype(jnp.bfloat16)
    rows_here, columns_here = scaled.shape
    row_ids = lax.axis_index("row") * rows_here + jnp.arange(rows_here, dtype=jnp.int32)
    column_ids = lax.axis_index("col") * columns_here + jnp.arange(columns_here, dtype=jnp.int32)
    identity = (row_ids[:, None] == column_ids[None, :]).astype(jnp.float32)
    scaled_rows = panel_rows(scaled)
    series = (identity + scaled.astype(jnp.float32) / 6.0).astype(jnp.bfloat16)
    for number in range(TERMS - 1):
        degree = TERMS - 1 - number
        series = (
            identity + expand(second_filters[number], panel_times(scaled_rows, series)) / degree
        ).astype(jnp.bfloat16)
    for number in range(SQUARINGS):
        series = expand(
            second_filters[TERMS - 1 + number], panel_times(panel_rows(series), series)
        ).astype(jnp.bfloat16)
    return series


def solution(mesh):
    return jax.shard_map(
        on_device,
        mesh=mesh,
        in_specs=(
            P("row", "col"),
            P("row", "col"),
            P("row", "col"),
            P(None, "row", "col"),
            P(None, "row", "col"),
            P(),
            P(None, "row", "col"),
        ),
        out_specs=P("row", "col"),
        check_vma=False,
    )
```

profile of v0, /device:TPU:0, one launch (start us, length us, event | category | flops | bytes accessed | tf_op | source)
XLA Modules:
  0.0 756.5 jit_solution(15816942738153316803)
XLA Ops:
  12.9 22.2 %all-gather.20.cloned.1.call-done = bf16[192,3072]{1,0:T(8,128)(2,1)} async-done(((bf16[192,384]{1,0:T(8,128)(2,1)}), bf16[192,3072]{1,0:T(8,128)(2,1)}) %all-gather.20.cloned.1.call-update) | async-done | bytes 1179664 | tf_op jit(solution)/shard_map/all_gather | solution.py:21
  35.1 47.9 %all-gather.22.cloned.1.call-done = bf16[3072,384]{1,0:T(8,128)(2,1)} async-done(((bf16[192,384]{1,0:T(8,128)(2,1)}), bf16[3072,384]{1,0:T(8,128)(2,1)}) %all-gather.22.cloned.1.call-update) | async-done | bytes 2359312 | tf_op jit(solution)/shard_map/all_gather | solution.py:27
  82.9 3.5 fusion.32
  90.3 17.1 %all-gather.28.cloned.1.call-done = bf16[192,3072]{1,0:T(8,128)(2,1)} async-done(((bf16[192,384]{1,0:T(8,128)(2,1)}), bf16[192,3072]{1,0:T(8,128)(2,1)}) %all-gather.28.cloned.1.call-update) | async-done | bytes 1179664 | tf_op jit(solution)/shard_map/all_gather | solution.py:21
  110.8 44.3 %all-gather.26.cloned.1.call-done = bf16[3072,384]{1,0:T(8,128)(2,1)} async-done(((bf16[192,384]{1,0:T(8,128)(2,1)}), bf16[3072,384]{1,0:T(8,128)(2,1)}) %all-gather.26.cloned.1.call-update) | async-done | bytes 2359312 | tf_op jit(solution)/shard_map/all_gather | solution.py:27
  155.1 24.3 %all-gather.24.cloned.1.call-done = bf16[192,3072]{1,0:T(8,128)(2,1)} async-done(((bf16[192,384]{1,0:T(8,128)(2,1)}), bf16[192,3072]{1,0:T(8,128)(2,1)}) %all-gather.24.cloned.1.call-update) | async-done | bytes 1179664 | tf_op jit(solution)/shard_map/all_gather | solution.py:21
  182.3 44.9 %all-gather.32.cloned.1.call-done = bf16[3072,384]{1,0:T(8,128)(2,1)} async-done(((bf16[192,384]{1,0:T(8,128)(2,1)}), bf16[3072,384]{1,0:T(8,128)(2,1)}) %all-gather.32.cloned.1.call-update) | async-done | bytes 2359312 | tf_op jit(solution)/shard_map/all_gather | solution.py:27
  227.2 24.5 %all-gather.30.cloned.1.call-done = bf16[192,3072]{1,0:T(8,128)(2,1)} async-done(((bf16[192,384]{1,0:T(8,128)(2,1)}), bf16[192,3072]{1,0:T(8,128)(2,1)}) %all-gather.30.cloned.1.call-update) | async-done | bytes 1179664 | tf_op jit(solution)/shard_map/all_gather | solution.py:21
  251.7 3.5 fusion.34
  255.3 45.7 %all-gather.34.cloned.1.call-done = bf16[3072,384]{1,0:T(8,128)(2,1)} async-done(((bf16[192,384]{1,0:T(8,128)(2,1)}), bf16[3072,384]{1,0:T(8,128)(2,1)}) %all-gather.34.cloned.1.call-update) | async-done | bytes 2359312 | tf_op jit(solution)/shard_map/all_gather | solution.py:41
  305.7 23.5 %all-gather.36.cloned.1.call-done = bf16[192,3072]{0,1:T(8,128)(2,1)} async-done(((bf16[192,384]{0,1:T(8,128)(2,1)}), bf16[192,3072]{0,1:T(8,128)(2,1)}) %all-gather.36.cloned.1.call-update) | async-done | bytes 1179664 | tf_op jit(solution)/shard_map/all_gather | solution.py:48
  335.0 22.0 %all-gather.38.cloned.1.call-done = bf16[192,3072]{0,1:T(8,128)(2,1)} async-done(((bf16[192,384]{0,1:T(8,128)(2,1)}), bf16[192,3072]{0,1:T(8,128)(2,1)}) %all-gather.38.cloned.1.call-update) | async-done | bytes 1179664 | tf_op jit(solution)/shard_map/all_gather | solution.py:21
  357.0 48.1 %all-gather.40.cloned.1.call-done = bf16[3072,384]{1,0:T(8,128)(2,1)} async-done(((bf16[192,384]{1,0:T(8,128)(2,1)}), bf16[3072,384]{1,0:T(8,128)(2,1)}) %all-gather.40.cloned.1.call-update) | async-done | bytes 2359312 | tf_op jit(solution)/shard_map/all_gather | solution.py:27
  405.1 3.6 fusion.31
  409.6 44.2 %all-gather.42.cloned.1.call-done = bf16[3072,384]{1,0:T(8,128)(2,1)} async-done(((bf16[192,384]{1,0:T(8,128)(2,1)}), bf16[3072,384]{1,0:T(8,128)(2,1)}) %all-gather.42.cloned.1.call-update) | async-done | bytes 2359312 | tf_op jit(solution)/shard_map/all_gather | solution.py:27
  457.7 44.4 %all-gather.44.cloned.1.call-done = bf16[3072,384]{1,0:T(8,128)(2,1)} async-done(((bf16[192,384]{1,0:T(8,128)(2,1)}), bf16[3072,384]{1,0:T(8,128)(2,1)}) %all-gather.44.cloned.1.call-update) | async-done | bytes 2359312 | tf_op jit(solution)/shard_map/all_gather | solution.py:27
  505.9 44.4 %all-gather.46.cloned.1.call-done = bf16[3072,384]{1,0:T(8,128)(2,1)} async-done(((bf16[192,384]{1,0:T(8,128)(2,1)}), bf16[3072,384]{1,0:T(8,128)(2,1)}) %all-gather.46.cloned.1.call-update) | async-done | bytes 2359312 | tf_op jit(solution)/shard_map/all_gather | solution.py:27
  554.1 44.4 %all-gather.48.cloned.1.call-done = bf16[3072,384]{1,0:T(8,128)(2,1)} async-done(((bf16[192,384]{1,0:T(8,128)(2,1)}), bf16[3072,384]{1,0:T(8,128)(2,1)}) %all-gather.48.cloned.1.call-update) | async-done | bytes 2359312 | tf_op jit(solution)/shard_map/all_gather | solution.py:27
  603.0 21.6 %all-gather.50.cloned.1.call-done = bf16[192,3072]{1,0:T(8,128)(2,1)} async-done(((bf16[192,384]{1,0:T(8,128)(2,1)}), bf16[192,3072]{1,0:T(8,128)(2,1)}) %all-gather.50.cloned.1.call-update) | async-done | bytes 1179664 | tf_op jit(solution)/shard_map/all_gather | solution.py:21
  624.6 47.7 %all-gather.52.cloned.1.call-done = bf16[3072,384]{1,0:T(8,128)(2,1)} async-done(((bf16[192,384]{1,0:T(8,128)(2,1)}), bf16[3072,384]{1,0:T(8,128)(2,1)}) %all-gather.52.cloned.1.call-update) | async-done | bytes 2359312 | tf_op jit(solution)/shard_map/all_gather | solution.py:27
  672.3 3.5 fusion.35
  677.2 21.5 %all-gather.54.cloned.1.call-done = bf16[192,3072]{1,0:T(8,128)(2,1)} async-done(((bf16[192,384]{1,0:T(8,128)(2,1)}), bf16[192,3072]{1,0:T(8,128)(2,1)}) %all-gather.54.cloned.1.call-update) | async-done | bytes 1179664 | tf_op jit(solution)/shard_map/all_gather | solution.py:21
  698.7 47.9 %all-gather.56.cloned.1.call-done = bf16[3072,384]{1,0:T(8,128)(2,1)} async-done(((bf16[192,384]{1,0:T(8,128)(2,1)}), bf16[3072,384]{1,0:T(8,128)(2,1)}) %all-gather.56.cloned.1.call-update) | async-done | bytes 2359312 | tf_op jit(solution)/shard_map/all_gather | solution.py:27
  746.5 3.5 fusion.36
  (109 shorter events, 44.9 us)
Async XLA Ops:
  6.5 28.5 %all-gather.20.cloned.1.call-start = ((), (), s32[]{:S(2)}) async-start(), calls=%async_computation | async-start | bytes 1327104 | tf_op jit(solution)/shard_map/all_gather | solution.py:21
  8.7 74.2 %all-gather.22.cloned.1.call-start = ((), (), s32[]{:S(2)}) async-start(), calls=%async_computation.1 | async-start | bytes 2506752 | tf_op jit(solution)/shard_map/all_gather | solution.py:27
  9.4 2.8 copy-start.5
  10.2 97.2 %all-gather.28.cloned.1.call-start = ((), (), s32[]{:S(2)}) async-start(), calls=%async_computation.4 | async-start | bytes 1327104 | tf_op jit(solution)/shard_map/all_gather | solution.py:21
  11.6 143.6 %all-gather.26.cloned.1.call-start = ((), (), s32[]{:S(2)}) async-start(), calls=%async_computation.3 | async-start | bytes 2506752 | tf_op jit(solution)/shard_map/all_gather | solution.py:27
  12.2 167.3 %all-gather.24.cloned.1.call-start = ((), (), s32[]{:S(2)}) async-start(), calls=%async_computation.2 | async-start | bytes 1327104 | tf_op jit(solution)/shard_map/all_gather | solution.py:21
  86.4 140.8 %all-gather.32.cloned.1.call-start = ((), (), s32[]{:S(2)}) async-start(), calls=%async_computation.6 | async-start | bytes 2506752 | tf_op jit(solution)/shard_map/all_gather | solution.py:27
  87.0 164.7 %all-gather.30.cloned.1.call-start = ((), (), s32[]{:S(2)}) async-start(), calls=%async_computation.5 | async-start | bytes 1327104 | tf_op jit(solution)/shard_map/all_gather | solution.py:21
  87.0 20.4 %copy-start = (bf16[3072,384]{1,0:T(8,128)(2,1)S(1)}, bf16[3072,384]{1,0:T(8,128)(2,1)}, u32[]{:S(2)}) copy-start(bf16[3072,384]{1,0:T(8,128)(2,1)} %all-gather.22.cloned.1.call-done) | copy-start | bytes 7077892
  110.1 190.8 %all-gather.34.cloned.1.call-start = ((), (), s32[]{:S(2)}) async-start(), calls=%async_computation.7 | async-start | bytes 2506752 | tf_op jit(solution)/shard_map/all_gather | solution.py:41
  182.3 73.0 %copy-start.7 = (s32[96]{0:T(128)S(1)}, s32[96]{0:T(128)}, u32[]{:S(2)}) copy-start(s32[96]{0:T(128)} %param.12) | copy-start | bytes 1156
  255.2 74.1 %all-gather.36.cloned.1.call-start = ((), (), s32[]{:S(2)}) async-start(), calls=%async_computation.8 | async-start | bytes 1769472 | tf_op jit(solution)/shard_map/all_gather | solution.py:48
  305.6 51.4 %all-gather.38.cloned.1.call-start = ((), (), s32[]{:S(2)}) async-start(), calls=%async_computation.9 | async-start | bytes 1769472 | tf_op jit(solution)/shard_map/all_gather | solution.py:21
  329.2 5.1 copy-start.4
  332.3 72.8 %all-gather.40.cloned.1.call-start = ((), (), s32[]{:S(2)}) async-start(), calls=%async_computation.10 | async-start | bytes 2506752 | tf_op jit(solution)/shard_map/all_gather | solution.py:27
  334.3 119.5 %all-gather.42.cloned.1.call-start = ((), (), s32[]{:S(2)}) async-start(), calls=%async_computation.11 | async-start | bytes 2506752 | tf_op jit(solution)/shard_map/all_gather | solution.py:27
  408.7 93.3 %all-gather.44.cloned.1.call-start = ((), (), s32[]{:S(2)}) async-start(), calls=%async_computation.12 | async-start | bytes 2506752 | tf_op jit(solution)/shard_map/all_gather | solution.py:27
  409.0 44.8 %copy-start.6 = (bf16[192,3072]{0,1:T(8,128)(2,1)S(1)}, bf16[192,3072]{0,1:T(8,128)(2,1)}, u32[]{:S(2)}) copy-start(bf16[192,3072]{0,1:T(8,128)(2,1)} %all-gather.38.cloned.1.call-done) | copy-start | bytes 3538948
  457.0 93.3 %all-gather.46.cloned.1.call-start = ((), (), s32[]{:S(2)}) async-start(), calls=%async_computation.13 | async-start | bytes 2506752 | tf_op jit(solution)/shard_map/all_gather | solution.py:27
  505.2 93.3 %all-gather.48.cloned.1.call-start = ((), (), s32[]{:S(2)}) async-start(), calls=%async_computation.14 | async-start | bytes 2506752 | tf_op jit(solution)/shard_map/all_gather | solution.py:27
  553.4 71.1 %all-gather.50.cloned.1.call-start = ((), (), s32[]{:S(2)}) async-start(), calls=%async_computation.15 | async-start | bytes 1327104 | tf_op jit(solution)/shard_map/all_gather | solution.py:21
  601.7 70.6 %all-gather.52.cloned.1.call-start = ((), (), s32[]{:S(2)}) async-start(), calls=%async_computation.16 | async-start | bytes 2506752 | tf_op jit(solution)/shard_map/all_gather | solution.py:27
  602.3 96.4 %all-gather.54.cloned.1.call-start = ((), (), s32[]{:S(2)}) async-start(), calls=%async_computation.17 | async-start | bytes 1327104 | tf_op jit(solution)/shard_map/all_gather | solution.py:21
  675.8 70.8 %all-gather.56.cloned.1.call-start = ((), (), s32[]{:S(2)}) async-start(), calls=%async_computation.18 | async-start | bytes 2506752 | tf_op jit(solution)/shard_map/all_gather | solution.py:27
  (3 other events, 5.3 us)
Sparse Core Ops, SparseCore 0:
  9.0 25.9 all-gather.19
  37.2 45.6 all-gather.21
  84.6 22.7 all-gather.27
  109.4 45.6 all-gather.25
  156.7 22.7 all-gather.23
  181.5 45.6 all-gather.31
  228.9 22.7 all-gather.29
  255.3 45.6 all-gather.33
  305.7 23.4 all-gather.35
  332.5 24.4 all-gather.37
  359.2 45.8 all-gather.39
  408.9 44.8 all-gather.41
  457.1 44.8 all-gather.43
  505.3 44.8 all-gather.45
  553.6 44.8 all-gather.47
  601.8 22.7 all-gather.49
  626.6 45.6 all-gather.51
  675.9 22.7 all-gather.53
  700.8 45.6 all-gather.55
where the time goes:
time: 757 us
  waiting for transfers between devices  683 us (90%)
  matrix products  38.5 us (5%)
  local copies, waits for them, and re-layouts  16.9 us (2%)
  between operations  13.7 us (2%)
    all_gather x10, waiting for transfers between devices, panel_times(): lax.all_gather(matrix, 'row', axis=0, tiled=True)  458 us
    all_gather x7, waiting for transfers between devices, panel_rows(): return lax.all_gather(matrix, 'col', axis=1, tiled=True)  153 us
    all_gather x1, waiting for transfers between devices, reorder(): segment = lax.all_gather(generator, 'row', axis=0, tiled=True)  45.7 us
    dot_general x11, matrix products, panel_times(): jnp.dot(row_panel, lax.all_gather(matrix, 'row', axis=0, tiled=True), pre...  35.6 us
    all_gather x1, waiting for transfers between devices, reorder(): segment = lax.all_gather(by_rows, 'col', axis=1, tiled=True)  23.5 us
  transfers between devices with their start and end apart: 19, of which 19 were waited for; matrix products, arithmetic and copies ran while one was open for 3% of the time, Pallas kernels for 0%

commit v1 on v0

--- a/solution.py
+++ b/solution.py
@@ -6,6 +6,24 @@
 BLK = 32
 TERMS = 6
 SQUARINGS = 2
+
+
+def ring_gather(shard, axis, dim):
+    ways, here, hop = (lax.axis_size(axis), lax.axis_index(axis), shard.shape[dim])
+    lengths = [n * ways if d == dim else n for d, n in enumerate(shard.shape)]
+    full = lax.dynamic_update_slice_in_dim(
+        jnp.zeros(lengths, shard.dtype), shard, here * hop, axis=dim
+    )
+    going_up = going_down = shard
+    for far in range(1, ways // 2 + 1):
+        going_up = lax.ppermute(going_up, axis, [(d, (d + 1) % ways) for d in range(ways)])
+        full = lax.dynamic_update_slice_in_dim(full, going_up, (here - far) % ways * hop, axis=dim)
+        if 2 * far < ways:
+            going_down = lax.ppermute(going_down, axis, [(d, (d - 1) % ways) for d in range(ways)])
+            full = lax.dynamic_update_slice_in_dim(
+                full, going_down, (here + far) % ways * hop, axis=dim
+            )
+    return full
 
 
 def expand(mask, values):
@@ -22,11 +40,7 @@
 
 
 def panel_times(row_panel, matrix):
-    return jnp.dot(
-        row_panel,
-        lax.all_gather(matrix, "row", axis=0, tiled=True),
-        preferred_element_type=jnp.float32,
-    )
+    return jnp.dot(row_panel, ring_gather(matrix, "row", 0), preferred_element_type=jnp.float32)
 
 
 def reorder(generator, owner_order):

time: 757 us -> 824 us (1.089); the launches traced: 757 us -> 815 us
  waiting for transfers between devices: 683 us -> 271 us
  starting transfers between devices: 0.93 us -> 379 us
  local copies, waits for them, and re-layouts: 16.9 us -> 121 us
  matrix products: 38.5 us -> 25.1 us
    all_gather x10 -> x0, waiting for transfers between devices: 458 us -> none  [panel_times(): lax.all_gather(matrix, 'row', axis=0, tiled=True)]
    ppermute x0 -> x150, starting transfers between devices: none -> 379 us  [the longest x70 370 us: ring_gather(): lax.ppermute(going_down, axis, [(d, (d - 1) % ways) for d in range(ways)])]
    ppermute x0 -> x150, waiting for transfers between devices: none -> 205 us  [the longest x80 201 us: ring_gather(): lax.ppermute(going_up, axis, [(d, (d + 1) % ways) for d in range(ways)])]
    all_gather x7, waiting for transfers between devices: 153 us -> 0.09 us  [panel_rows(): return lax.all_gather(matrix, 'col', axis=1, tiled=True)]
    dynamic_update_slice x0 -> x150, local copies, waits for them, and re-layouts: none -> 80.6 us  [the longest x80 42.5 us: ring_gather(): lax.dynamic_update_slice_in_dim(full, going_up, (here - far) % ways * hop...]
    dot_general x11, matrix products: 35.6 us -> 22.2 us  [panel_times(): jnp.dot(row_panel, ring_gather(matrix, 'row', 0), preferred_element_type=...]
    mul x26, local copies, waits for them, and re-layouts: 10.8 us -> 21.2 us  [expand(): values.reshape(row_blocks, BLK, column_blocks, BLK)]
    unnamed x16 -> x52, local copies, waits for them, and re-layouts: 0.04 us -> 10.3 us
  transfers between devices with their start and end apart: 19 -> 159, of which waited for: 19 -> 78; matrix products, arithmetic and copies ran while one was open for 3% -> 14% of each run, Pallas kernels for 0% -> 0%
where the time goes in v1:
time: 824 us; the launch traced here: 815 us
  starting transfers between devices  379 us (46%)
  waiting for transfers between devices  271 us (33%)
  local copies, waits for them, and re-layouts  121 us (15%)
  matrix products  25.1 us (3%)
  between operations  15 us (2%)
    ppermute x70, starting transfers between devices, ring_gather(): lax.ppermute(going_down, axis, [(d, (d - 1) % ways) for d in range(ways)])  370 us
    ppermute x80, waiting for transfers between devices, ring_gather(): lax.ppermute(going_up, axis, [(d, (d + 1) % ways) for d in range(ways)])  201 us
    all_gather x1, waiting for transfers between devices, reorder(): segment = lax.all_gather(generator, 'row', axis=0, tiled=True)  42.5 us
    dynamic_update_slice x80, local copies, waits for them, and re-layouts, ring_gather(): lax.dynamic_update_slice_in_dim(full, going_up, (here - far) % ways * hop...  42.5 us
    dynamic_update_slice x70, local copies, waits for them, and re-layouts, ring_gather(): lax.dynamic_update_slice_in_dim(full, going_down, (here + far) % ways * h...  38.1 us
    all_gather x1, waiting for transfers between devices, reorder(): segment = lax.all_gather(by_rows, 'col', axis=1, tiled=True)  23.5 us
    dot_general x11, matrix products, panel_times(): jnp.dot(row_panel, ring_gather(matrix, 'row', 0), preferred_element_type=...  22.2 us
    mul x26, local copies, waits for them, and re-layouts, expand(): values.reshape(row_blocks, BLK, column_blocks, BLK)  21.2 us
  transfers between devices with their start and end apart: 159, of which 78 were waited for; matrix products, arithmetic and copies ran while one was open for 14% of the time, Pallas kernels for 0%

profile of v1, /device:TPU:0, one launch (start us, length us, event | category | flops | bytes accessed | tf_op | source)
XLA Modules:
  0.0 815.2 jit_solution(6855958698867075641)
XLA Ops:
  69.6 5.6 collective-permute-start.13
  79.4 8.4 %collective-permute-done.14 = bf16[192,384]{1,0:T(8,128)(2,1)S(1)} collective-permute-done((bf16[192,384]{1,0:T(8,128)(2,1)S(1)}, bf16[192,384]{1,0:T(8,128)(2,1)S(1)}, u32[]{:S(2)}, u32[]{:S(2)}) %collective-permute-start.14) | collective-permute-done | bytes 147488 | tf_op jit(solution)/shard_map/ppermute | solution.py:19
  210.2 42.5 %all-gather.18.cloned.1.call-done = bf16[3072,384]{1,0:T(8,128)(2,1)} async-done(((bf16[192,384]{1,0:T(8,128)(2,1)}), bf16[3072,384]{1,0:T(8,128)(2,1)}) %all-gather.18.cloned.1.call-update) | async-done | bytes 2359312 | tf_op jit(solution)/shard_map/all_gather | solution.py:55
  257.5 23.5 %all-gather.20.cloned.1.call-done = bf16[192,3072]{0,1:T(8,128)(2,1)} async-done(((bf16[192,384]{0,1:T(8,128)(2,1)}), bf16[192,3072]{0,1:T(8,128)(2,1)}) %all-gather.20.cloned.1.call-update) | async-done | bytes 1179664 | tf_op jit(solution)/shard_map/all_gather | solution.py:62
  337.1 5.6 collective-permute-start.58
  347.5 7.1 collective-permute-done.59
  421.9 7.7 collective-permute-done.74
  468.9 5.6 collective-permute-start.84
  487.1 5.8 collective-permute-start.88
  497.3 7.6 collective-permute-done.89
  525.9 5.6 collective-permute-start.95
  535.8 5.7 collective-permute-start.97
  553.8 5.8 collective-permute-start.101
  563.5 5.8 collective-permute-start.103
  573.1 7.3 collective-permute-done.104
  602.6 5.6 collective-permute-start.110
  628.9 5.8 collective-permute-start.116
  638.9 5.8 collective-permute-start.118
  648.7 7.3 collective-permute-done.119
  696.1 5.7 collective-permute-start.129
  704.7 5.8 collective-permute-start.131
  714.5 5.8 collective-permute-start.133
  723.7 8.5 %collective-permute-done.134 = bf16[192,384]{1,0:T(8,128)(2,1)S(1)} collective-permute-done((bf16[192,384]{1,0:T(8,128)(2,1)S(1)}, bf16[192,384]{1,0:T(8,128)(2,1)S(1)}, u32[]{:S(2)}, u32[]{:S(2)}) %collective-permute-start.134) | collective-permute-done | bytes 147488 | tf_op jit(solution)/shard_map/ppermute | solution.py:19
  797.0 8.4 %collective-permute-done.149 = bf16[192,384]{1,0:T(8,128)(2,1)S(1)} collective-permute-done((bf16[192,384]{1,0:T(8,128)(2,1)S(1)}, bf16[192,384]{1,0:T(8,128)(2,1)S(1)}, u32[]{:S(2)}, u32[]{:S(2)}) %collective-permute-start.149) | collective-permute-done | bytes 147488 | tf_op jit(solution)/shard_map/ppermute | solution.py:19
  (575 shorter events, 592.0 us)
Async XLA Ops:
  6.5 81.3 %all-gather.14.cloned.1.call-start = ((), (), s32[]{:S(2)}) async-start(), calls=%async_computation.2 | async-start | bytes 1327104 | tf_op jit(solution)/shard_map/all_gather | solution.py:39
  10.3 143.3 %all-gather.10.cloned.1.call-start = ((), (), s32[]{:S(2)}) async-start(), calls=%async_computation | async-start | bytes 1327104 | tf_op jit(solution)/shard_map/all_gather | solution.py:39
  10.4 92.5 %collective-permute-start.15 = (bf16[192,384]{1,0:T(8,128)(2,1)}, bf16[192,384]{1,0:T(8,128)(2,1)S(1)}, u32[]{:S(2)}, u32[]{:S(2)}) collective-permute-start(bf16[192,384]{1,0:T(8,128)(2,1)} %get-tuple-element.8), channel_id=1, source_target_pairs={{0,8},{8,16},{16,24},{24,32},{32,40},{40,48},{48,56},{56,64},{64,7... | collective-permute-start | bytes 442376 | tf_op jit(solution)/shard_map/ppermute | solution.py:19
  22.5 181.2 %all-gather.16.cloned.1.call-start = ((), (), s32[]{:S(2)}) async-start(), calls=%async_computation.3 | async-start | bytes 1327104 | tf_op jit(solution)/shard_map/all_gather | solution.py:39
  90.6 115.9 %all-gather.12.cloned.1.call-start = ((), (), s32[]{:S(2)}) async-start(), calls=%async_computation.1 | async-start | bytes 1327104 | tf_op jit(solution)/shard_map/all_gather | solution.py:39
  90.8 19.9 %collective-permute-start.30 = (bf16[192,384]{1,0:T(8,128)(2,1)S(1)}, bf16[192,384]{1,0:T(8,128)(2,1)}, u32[]{:S(2)}, u32[]{:S(2)}) collective-permute-start(bf16[192,384]{1,0:T(8,128)(2,1)S(1)} %copy-done.14), channel_id=1, source_target_pairs={{0,8},{8,16},{16,24},{24,32},{32,40},{40,48},{48,56},{56,64},{64,7... | collective-permute-start | bytes 442376 | tf_op jit(solution)/shard_map/ppermute | solution.py:19
  92.8 19.5 %collective-permute-start.31 = (bf16[192,384]{1,0:T(8,128)(2,1)S(1)}, bf16[192,384]{1,0:T(8,128)(2,1)}, u32[]{:S(2)}, u32[]{:S(2)}) collective-permute-start(bf16[192,384]{1,0:T(8,128)(2,1)S(1)} %copy-done.14), channel_id=1, source_target_pairs={{0,120},{8,0},{16,8},{24,16},{32,24},{40,32},{48,40},{56,48},{64,5... | collective-permute-start | bytes 442376 | tf_op jit(solution)/shard_map/ppermute | solution.py:22
  102.9 16.3 %collective-permute-start.17 = (bf16[192,384]{1,0:T(8,128)(2,1)S(1)}, bf16[192,384]{1,0:T(8,128)(2,1)S(1)}, u32[]{:S(2)}, u32[]{:S(2)}) collective-permute-start(bf16[192,384]{1,0:T(8,128)(2,1)S(1)} %collective-permute-done.15), channel_id=1, source_target_pairs={{0,8},{8,16},{16,24},{24,32},{32,40},{40,48},{48,56},{56,64},{64,7... | collective-permute-start | bytes 442376 | tf_op jit(solution)/shard_map/ppermute | solution.py:19
  103.7 16.2 %collective-permute-start.18 = (bf16[192,384]{1,0:T(8,128)(2,1)}, bf16[192,384]{1,0:T(8,128)(2,1)S(1)}, u32[]{:S(2)}, u32[]{:S(2)}) collective-permute-start(bf16[192,384]{1,0:T(8,128)(2,1)} %collective-permute-done.16), channel_id=1, source_target_pairs={{0,120},{8,0},{16,8},{24,16},{32,24},{40,32},{48,40},{56,48},{64,5... | collective-permute-start | bytes 442376 | tf_op jit(solution)/shard_map/ppermute | solution.py:22
  110.7 15.3 %collective-permute-start.32 = (bf16[192,384]{1,0:T(8,128)(2,1)}, bf16[192,384]{1,0:T(8,128)(2,1)S(1)}, u32[]{:S(2)}, u32[]{:S(2)}) collective-permute-start(bf16[192,384]{1,0:T(8,128)(2,1)} %collective-permute-done.30), channel_id=1, source_target_pairs={{0,8},{8,16},{16,24},{24,32},{32,40},{40,48},{48,56},{56,64},{64,7... | collective-permute-start | bytes 442376 | tf_op jit(solution)/shard_map/ppermute | solution.py:19
  112.3 14.3 %collective-permute-start.33 = (bf16[192,384]{1,0:T(8,128)(2,1)}, bf16[192,384]{1,0:T(8,128)(2,1)S(1)}, u32[]{:S(2)}, u32[]{:S(2)}) collective-permute-start(bf16[192,384]{1,0:T(8,128)(2,1)} %collective-permute-done.31), channel_id=1, source_target_pairs={{0,120},{8,0},{16,8},{24,16},{32,24},{40,32},{48,40},{56,48},{64,5... | collective-permute-start | bytes 442376 | tf_op jit(solution)/shard_map/ppermute | solution.py:22
  126.6 13.4 %collective-permute-start.35 = (bf16[192,384]{1,0:T(8,128)(2,1)S(1)}, bf16[192,384]{1,0:T(8,128)(2,1)S(1)}, u32[]{:S(2)}, u32[]{:S(2)}) collective-permute-start(bf16[192,384]{1,0:T(8,128)(2,1)S(1)} %collective-permute-done.33), channel_id=1, source_target_pairs={{0,120},{8,0},{16,8},{24,16},{32,24},{40,32},{48,40},{56,48},{64,5... | collective-permute-start | bytes 442376 | tf_op jit(solution)/shard_map/ppermute | solution.py:22
  140.1 18.0 %collective-permute-start.37 = (bf16[192,384]{1,0:T(8,128)(2,1)S(1)}, bf16[192,384]{1,0:T(8,128)(2,1)}, u32[]{:S(2)}, u32[]{:S(2)}) collective-permute-start(bf16[192,384]{1,0:T(8,128)(2,1)S(1)} %collective-permute-done.35), channel_id=1, source_target_pairs={{0,120},{8,0},{16,8},{24,16},{32,24},{40,32},{48,40},{56,48},{64,5... | collective-permute-start | bytes 442376 | tf_op jit(solution)/shard_map/ppermute | solution.py:22
  146.1 19.0 %collective-permute-start.23 = (bf16[192,384]{1,0:T(8,128)(2,1)S(1)}, bf16[192,384]{1,0:T(8,128)(2,1)}, u32[]{:S(2)}, u32[]{:S(2)}) collective-permute-start(bf16[192,384]{1,0:T(8,128)(2,1)S(1)} %collective-permute-done.21), channel_id=1, source_target_pairs={{0,8},{8,16},{16,24},{24,32},{32,40},{40,48},{48,56},{56,64},{64,7... | collective-permute-start | bytes 442376 | tf_op jit(solution)/shard_map/ppermute | solution.py:19
  146.1 20.6 %collective-permute-start.24 = (bf16[192,384]{1,0:T(8,128)(2,1)}, bf16[192,384]{1,0:T(8,128)(2,1)S(1)}, u32[]{:S(2)}, u32[]{:S(2)}) collective-permute-start(bf16[192,384]{1,0:T(8,128)(2,1)} %collective-permute-done.22), channel_id=1, source_target_pairs={{0,120},{8,0},{16,8},{24,16},{32,24},{40,32},{48,40},{56,48},{64,5... | collective-permute-start | bytes 442376 | tf_op jit(solution)/shard_map/ppermute | solution.py:22
  151.4 21.2 %collective-permute-start.38 = (bf16[192,384]{1,0:T(8,128)(2,1)}, bf16[192,384]{1,0:T(8,128)(2,1)S(1)}, u32[]{:S(2)}, u32[]{:S(2)}) collective-permute-start(bf16[192,384]{1,0:T(8,128)(2,1)} %collective-permute-done.36), channel_id=1, source_target_pairs={{0,8},{8,16},{16,24},{24,32},{32,40},{40,48},{48,56},{56,64},{64,7... | collective-permute-start | bytes 442376 | tf_op jit(solution)/shard_map/ppermute | solution.py:19
  156.4 96.3 %all-gather.18.cloned.1.call-start = ((), (), s32[]{:S(2)}) async-start(), calls=%async_computation.4 | async-start | bytes 2506752 | tf_op jit(solution)/shard_map/all_gather | solution.py:55
  158.0 15.3 %collective-permute-start.39 = (bf16[192,384]{1,0:T(8,128)(2,1)}, bf16[192,384]{1,0:T(8,128)(2,1)S(1)}, u32[]{:S(2)}, u32[]{:S(2)}) collective-permute-start(bf16[192,384]{1,0:T(8,128)(2,1)} %collective-permute-done.37), channel_id=1, source_target_pairs={{0,120},{8,0},{16,8},{24,16},{32,24},{40,32},{48,40},{56,48},{64,5... | collective-permute-start | bytes 442376 | tf_op jit(solution)/shard_map/ppermute | solution.py:22
  165.0 14.3 %collective-permute-start.25 = (bf16[192,384]{1,0:T(8,128)(2,1)}, bf16[192,384]{1,0:T(8,128)(2,1)S(1)}, u32[]{:S(2)}, u32[]{:S(2)}) collective-permute-start(bf16[192,384]{1,0:T(8,128)(2,1)} %collective-permute-done.23), channel_id=1, source_target_pairs={{0,8},{8,16},{16,24},{24,32},{32,40},{40,48},{48,56},{56,64},{64,7... | collective-permute-start | bytes 442376 | tf_op jit(solution)/shard_map/ppermute | solution.py:19
  180.0 15.2 %collective-permute-start.28 = (bf16[192,384]{1,0:T(8,128)(2,1)S(1)}, bf16[192,384]{1,0:T(8,128)(2,1)S(1)}, u32[]{:S(2)}, u32[]{:S(2)}) collective-permute-start(bf16[192,384]{1,0:T(8,128)(2,1)S(1)} %collective-permute-done.26), channel_id=1, source_target_pairs={{0,120},{8,0},{16,8},{24,16},{32,24},{40,32},{48,40},{56,48},{64,5... | collective-permute-start | bytes 442376 | tf_op jit(solution)/shard_map/ppermute | solution.py:22
  210.0 70.9 %all-gather.20.cloned.1.call-start = ((), (), s32[]{:S(2)}) async-start(), calls=%async_computation.5 | async-start | bytes 1769472 | tf_op jit(solution)/shard_map/all_gather | solution.py:62
  257.3 97.9 %all-gather.22.cloned.1.call-start = ((), (), s32[]{:S(2)}) async-start(), calls=%async_computation.6 | async-start | bytes 1769472 | tf_op jit(solution)/shard_map/all_gather | solution.py:39
  284.1 448.2 %all-gather.24.cloned.1.call-start = ((), (), s32[]{:S(2)}) async-start(), calls=%async_computation.7 | async-start | bytes 1327104 | tf_op jit(solution)/shard_map/all_gather | solution.py:39
  659.9 145.6 %all-gather.26.cloned.1.call-start = ((), (), s32[]{:S(2)}) async-start(), calls=%async_computation.8 | async-start | bytes 1327104 | tf_op jit(solution)/shard_map/all_gather | solution.py:39
  (161 other events, 1472.3 us)
Sparse Core Ops, SparseCore 0:
  10.5 25.9 all-gather.13
  38.2 23.4 all-gather.9
  90.7 19.7 all-gather.15
  156.5 24.5 all-gather.11
  210.2 42.4 all-gather.17
  257.4 23.4 all-gather.19
  284.2 24.4 all-gather.21
  660.0 18.7 all-gather.23
  736.6 18.7 all-gather.25
